TPU v7x, 32 devices: a whole 2x2x4 slice. The times are simulated.
32 devices in a mesh: group: 4 (over y, x), member: 8 (over z, core).
Axes of the slice: x: 2, y: 2, z: 4, core: 2. Of those that a mesh axis runs over, the one named last changes fastest.
Arguments:
- activations: bfloat16 [4, 1024, 2048], P('group', 'member'), may hold values from -6 to 6
- lengths: int32 [4, 8], P('group'), may hold values from 1 to 128, 576 in all within a row
- assignment: int32 [4, 8], P('group'), may hold values from 0 to 7, each once within a row
- owners: int32 [4], replicated, may hold values from 0 to 3
- prefix_cache: bfloat16 [4, 8192, 256], P('group', 'member'), may hold values from -244 to 244
- first_gain: float32 [2048], replicated, may hold values from 0.1 to 1.9
- first_bias: float32 [2048], replicated, may hold values from -3 to 3
- query_weight: bfloat16 [2048, 2048], replicated, may hold values from -0.125 to 0.125
- keyval_weight: bfloat16 [2048, 256], replicated, may hold values from -0.4375 to 0.4375
- output_weight: bfloat16 [2048, 2048], replicated, may hold values from -0.125 to 0.125
- second_gain: float32 [2048], replicated, may hold values from 0.1 to 1.9
- second_bias: float32 [2048], replicated, may hold values from -3 to 3
- expand_weight: bfloat16 [2048, 8192], P(None, 'member'), may hold values from -0.125 to 0.125
- contract_weight: bfloat16 [8192, 2048], P('member'), may hold values from -0.0625 to 0.0625
Outputs:
- layer_output: bfloat16 [4, 1024, 2048], P('group', 'member')
Inputs may be any that keep to these rules, and one draw needn't show every extreme that they name: Each row of lengths sums to 576 and its longest entry is 128. Each row of assignment names every request of its group once. `owners`: several groups may attend the same cache slot.
All inputs are finite; a program needn't handle non-finite values.
Results may differ from a plain program's by a relative error of at most 0.011.
The roundings to bfloat16 on the way count: a program that leaves them out, or rounds other values in their place, can miss the bound.
Values may be sent and summed in bfloat16 or wider, within the bound.
No kernel may reach another device: no remote copies, remote signals or barrier semaphores. Data moves between devices by JAX's collectives and lax.ppermute only.
A program may use at most 128 MiB of HBM per device.

v0:
```python
import math
import jax
import jax.numpy as jnp
from jax import lax
from jax.sharding import PartitionSpec as P

EPSILON = 1e-05
NEGATIVE = -1e30


def layer_norm(values, gain, bias):
    average = jnp.mean(values, axis=-1, keepdims=True)
    centered = values - average
    spread = jnp.mean(centered * centered, axis=-1, keepdims=True)
    return centered * lax.rsqrt(spread + EPSILON) * gain + bias


def pick_value(table, wanted):
    slots_at = lax.broadcasted_iota(jnp.int32, table.shape, 0)
    return jnp.sum(jnp.where(slots_at == wanted, table, 0))


def own_scores(query_block, own_keys, scaling):
    scores = (
        jnp.einsum("thd,sd->ths", query_block, own_keys, preferred_element_type=jnp.float32)
        * scaling
    )
    block_rows = query_block.shape[0]
    key_rows = own_keys.shape[0]
    row_at = lax.broadcasted_iota(jnp.int32, (block_rows, 1, key_rows), 0)
    column_at = lax.broadcasted_iota(jnp.int32, (block_rows, 1, key_rows), 2)
    return jnp.where(column_at <= row_at, scores, NEGATIVE)


def folded_attention(queries, keys_values, selected):
    row_count, head_count, head_size = queries.shape
    scaling = 1.0 / math.sqrt(head_size)
    own_keys = keys_values[:, :head_size]
    own_values = keys_values[:, head_size:]
    suffix_scores = own_scores(queries, own_keys, scaling)
    highest = jnp.max(suffix_scores, axis=-1)
    suffix_exp = jnp.exp(suffix_scores - highest[..., None])
    denominator = jnp.sum(suffix_exp, axis=-1)
    weighted = jnp.einsum(
        "ths,sd->thd",
        suffix_exp.astype(jnp.bfloat16),
        own_values,
        preferred_element_type=jnp.float32,
    )
    running = (weighted, highest, denominator)
    portion = lax.all_gather(selected, "member", axis=0, tiled=True)
    extent = portion.shape[0]
    stride = math.gcd(extent, 1024)

    def advance(state_now, block_index):
        weighted_now, highest_now, denominator_now = state_now
        key_block = lax.dynamic_slice_in_dim(portion, block_index * stride, stride, 0)
        scores = (
            jnp.einsum(
                "thd,pd->thp", queries, key_block[:, :head_size], preferred_element_type=jnp.float32
            )
            * scaling
        )
        highest_next = jnp.maximum(highest_now, jnp.max(scores, axis=-1))
        rescale = jnp.exp(highest_now - highest_next)
        exponent = jnp.exp(scores - highest_next[..., None])
        denominator_next = denominator_now * rescale + jnp.sum(exponent, axis=-1)
        weighted_next = weighted_now * rescale[..., None] + jnp.einsum(
            "thp,pd->thd",
            exponent.astype(jnp.bfloat16),
            key_block[:, head_size:],
            preferred_element_type=jnp.float32,
        )
        return ((weighted_next, highest_next, denominator_next), None)

    running, _ = lax.scan(advance, running, jnp.arange(extent // stride, dtype=jnp.int32))
    weighted, highest, denominator = running
    return (
        (weighted / denominator[..., None])
        .astype(jnp.bfloat16)
        .reshape(row_count, head_count * head_size)
    )


def shards(
    activations,
    lengths,
    assignment,
    owners,
    prefix_cache,
    first_gain,
    first_bias,
    query_weight,
    keyval_weight,
    output_weight,
    second_gain,
    second_bias,
    expand_weight,
    contract_weight,
):
    group_index = lax.axis_index("group")
    member_index = lax.axis_index("member")
    request = pick_value(assignment[0], member_index)
    length_here = pick_value(lengths[0], request)
    owner_here = pick_value(owners, group_index)
    tokens = activations[0]
    row_count = tokens.shape[0]
    head_size = prefix_cache.shape[2] // 2
    head_count = tokens.shape[1] // head_size
    every_block = lax.all_gather(prefix_cache, "group", axis=0, tiled=True)
    selected = lax.dynamic_index_in_dim(every_block, owner_here, 0, keepdims=False)
    tokens_wide = tokens.astype(jnp.float32)
    normed = layer_norm(tokens_wide, first_gain, first_bias).astype(jnp.bfloat16)
    queries = jnp.dot(normed, query_weight, preferred_element_type=jnp.float32).astype(jnp.bfloat16)
    queries = queries.reshape(row_count, head_count, head_size)
    keys_values = jnp.dot(normed, keyval_weight, preferred_element_type=jnp.float32).astype(
        jnp.bfloat16
    )
    attended = folded_attention(queries, keys_values, selected)
    residual = tokens_wide + jnp.dot(attended, output_weight, preferred_element_type=jnp.float32)
    second = layer_norm(residual, second_gain, second_bias).astype(jnp.bfloat16)
    hidden = jax.nn.gelu(
        jnp.dot(
            lax.all_gather(second, "member", axis=0, tiled=True),
            expand_weight,
            preferred_element_type=jnp.float32,
        ),
        approximate=True,
    ).astype(jnp.bfloat16)
    summed = lax.psum_scatter(
        jnp.dot(hidden, contract_weight, preferred_element_type=jnp.float32).astype(jnp.bfloat16),
        "member",
        scatter_dimension=0,
        tiled=True,
    ).astype(jnp.float32)
    is_live = lax.broadcasted_iota(jnp.int32, (row_count, 1), 0) < length_here
    return jnp.where(is_live, residual + summed, 0.0).astype(jnp.bfloat16)[None]


def solution(mesh):
    return jax.shard_map(
        shards,
        mesh=mesh,
        in_specs=(
            P("group", "member", None),
            P("group", None),
            P("group", None),
            P(),
            P("group", "member", None),
            P(),
            P(),
            P(),
            P(),
            P(),
            P(),
            P(),
            P(None, "member"),
            P("member", None),
        ),
        out_specs=P("group", "member", None),
        check_vma=False,
    )
```

profile of v0, /device:TPU:0, one launch (start us, length us, event | category | flops | bytes accessed | tf_op | source)
XLA Modules:
  0.0 286.6 jit_solution(2638500522030421383)
XLA Ops:
  10.5 36.7 %all-gather.5.cloned.1.call-done = bf16[4,1024,256]{2,1,0:T(8,128)(2,1)} async-done(((bf16[1,1024,256]{2,1,0:T(8,128)(2,1)}), bf16[4,1024,256]{2,1,0:T(8,128)(2,1)}) %all-gather.5.cloned.1.call-update) | async-done | bytes 2097168 | tf_op jit(solution)/shard_map/all_gather | solution.py:110
  47.2 1.9 constant_dynamic-slice_fusion
  51.8 5.0 %fusion.30 = bf16[16,16,8,128]{3,2,1,0:T(8,128)(2,1)S(1)} fusion(bf16[2048,2048]{1,0:T(8,128)(2,1)} %param.23, bf16[1,128,2048]{2,1,0:T(8,128)(2,1)} %param.16, f32[2048]{0:T(1024)} %param.22, f32[2048]{0:T(1024)} %param.21, f32[128]{0:T(128)S(1)} %add_rsqrt_fusion.1, f32[128]{0:T(128)S(1)} %broadcast_multiply_fusion.1), kind=kOutput, calls=%fused_computation.39 | convolution fusion | flops 1075576832 | bytes 9454592 | tf_op jit(solution)/shard_map/dot_general | solution.py:114
  58.2 38.3 %all-gather.9.cloned.1.call-done = bf16[1,8192,256]{2,1,0:T(8,128)(2,1)} async-done(((bf16[1,1024,256]{2,1,0:T(8,128)(2,1)}), bf16[1,8192,256]{2,1,0:T(8,128)(2,1)}) %all-gather.9.cloned.1.call-update) | async-done | bytes 4194320 | tf_op jit(solution)/shard_map/all_gather | solution.py:51
  96.4 62.7 %while.14 = (s32[]{:T(128)}, f32[128,16,128]{2,0,1:T(8,128)S(1)}, f32[128,16]{0,1:T(8,128)S(1)}, f32[128,16]{0,1:T(8,128)S(1)}, s32[8]{0:T(128)S(1)}, /*index=5*...) while((s32[]{:T(128)}, f32[128,16,128]{2,0,1:T(8,128)S(1)}, ...), condition=%wide.region_10.11_spmd, body=%wide.region_7.10_spmd.sunk | while | flops 1091047424 | bytes 28442832 | solution.py:76
  97.7 2.2 bitcast_reduce_fusion.2
  99.9 1.4 fusion.68
  101.3 2.9 %fusion.69 = f32[128,16,128]{2,0,1:T(8,128)S(1)} fusion(f32[1024,128,16]{1,0,2:T(8,128)S(1)} %get-tuple-element.135, f32[128,16]{0,1:T(8,128)S(1)} %max.4, f32[128,16,128]{2,0,1:T(8,128)S(1)} %get-tuple-element.152, f32[128,16]{0,1:T(8,128)S(1)} %get-tuple-element.137, bf16[8192,256]{1,0:T(8,128)(2,1)} %get-tuple-element.168, s32[]{:T(128)S(6)} %select_n.46, ...), kind=kOutput, calls=%fused_computation.8.clone.1 | convolution fusion | flops 543686656 | bytes 10764296 | tf_op jit(solution)/shard_map/while/body/eval_jaxpr/thp,pd->thd/dot_general | solution.py:68
  105.5 2.2 bitcast_reduce_fusion.2
  107.8 1.4 fusion.68
  109.2 2.9 %fusion.69 = f32[128,16,128]{2,0,1:T(8,128)S(1)} fusion(f32[1024,128,16]{1,0,2:T(8,128)S(1)} %get-tuple-element.135, f32[128,16]{0,1:T(8,128)S(1)} %max.4, f32[128,16,128]{2,0,1:T(8,128)S(1)} %get-tuple-element.152, f32[128,16]{0,1:T(8,128)S(1)} %get-tuple-element.137, bf16[8192,256]{1,0:T(8,128)(2,1)} %get-tuple-element.168, s32[]{:T(128)S(6)} %select_n.46, ...), kind=kOutput, calls=%fused_computation.8.clone.1 | convolution fusion | flops 543686656 | bytes 10764296 | tf_op jit(solution)/shard_map/while/body/eval_jaxpr/thp,pd->thd/dot_general | solution.py:68
  113.4 2.2 bitcast_reduce_fusion.2
  115.6 1.4 fusion.68
  117.0 2.9 %fusion.69 = f32[128,16,128]{2,0,1:T(8,128)S(1)} fusion(f32[1024,128,16]{1,0,2:T(8,128)S(1)} %get-tuple-element.135, f32[128,16]{0,1:T(8,128)S(1)} %max.4, f32[128,16,128]{2,0,1:T(8,128)S(1)} %get-tuple-element.152, f32[128,16]{0,1:T(8,128)S(1)} %get-tuple-element.137, bf16[8192,256]{1,0:T(8,128)(2,1)} %get-tuple-element.168, s32[]{:T(128)S(6)} %select_n.46, ...), kind=kOutput, calls=%fused_computation.8.clone.1 | convolution fusion | flops 543686656 | bytes 10764296 | tf_op jit(solution)/shard_map/while/body/eval_jaxpr/thp,pd->thd/dot_general | solution.py:68
  121.2 2.2 bitcast_reduce_fusion.2
  123.4 1.4 fusion.68
  124.8 2.9 %fusion.69 = f32[128,16,128]{2,0,1:T(8,128)S(1)} fusion(f32[1024,128,16]{1,0,2:T(8,128)S(1)} %get-tuple-element.135, f32[128,16]{0,1:T(8,128)S(1)} %max.4, f32[128,16,128]{2,0,1:T(8,128)S(1)} %get-tuple-element.152, f32[128,16]{0,1:T(8,128)S(1)} %get-tuple-element.137, bf16[8192,256]{1,0:T(8,128)(2,1)} %get-tuple-element.168, s32[]{:T(128)S(6)} %select_n.46, ...), kind=kOutput, calls=%fused_computation.8.clone.1 | convolution fusion | flops 543686656 | bytes 10764296 | tf_op jit(solution)/shard_map/while/body/eval_jaxpr/thp,pd->thd/dot_general | solution.py:68
  129.0 2.2 bitcast_reduce_fusion.2
  131.3 1.4 fusion.68
  132.7 2.9 %fusion.69 = f32[128,16,128]{2,0,1:T(8,128)S(1)} fusion(f32[1024,128,16]{1,0,2:T(8,128)S(1)} %get-tuple-element.135, f32[128,16]{0,1:T(8,128)S(1)} %max.4, f32[128,16,128]{2,0,1:T(8,128)S(1)} %get-tuple-element.152, f32[128,16]{0,1:T(8,128)S(1)} %get-tuple-element.137, bf16[8192,256]{1,0:T(8,128)(2,1)} %get-tuple-element.168, s32[]{:T(128)S(6)} %select_n.46, ...), kind=kOutput, calls=%fused_computation.8.clone.1 | convolution fusion | flops 543686656 | bytes 10764296 | tf_op jit(solution)/shard_map/while/body/eval_jaxpr/thp,pd->thd/dot_general | solution.py:68
  136.9 2.2 bitcast_reduce_fusion.2
  139.1 1.4 fusion.68
  140.5 2.9 %fusion.69 = f32[128,16,128]{2,0,1:T(8,128)S(1)} fusion(f32[1024,128,16]{1,0,2:T(8,128)S(1)} %get-tuple-element.135, f32[128,16]{0,1:T(8,128)S(1)} %max.4, f32[128,16,128]{2,0,1:T(8,128)S(1)} %get-tuple-element.152, f32[128,16]{0,1:T(8,128)S(1)} %get-tuple-element.137, bf16[8192,256]{1,0:T(8,128)(2,1)} %get-tuple-element.168, s32[]{:T(128)S(6)} %select_n.46, ...), kind=kOutput, calls=%fused_computation.8.clone.1 | convolution fusion | flops 543686656 | bytes 10764296 | tf_op jit(solution)/shard_map/while/body/eval_jaxpr/thp,pd->thd/dot_general | solution.py:68
  144.7 2.2 bitcast_reduce_fusion.2
  148.4 2.9 %fusion.69 = f32[128,16,128]{2,0,1:T(8,128)S(1)} fusion(f32[1024,128,16]{1,0,2:T(8,128)S(1)} %get-tuple-element.135, f32[128,16]{0,1:T(8,128)S(1)} %max.4, f32[128,16,128]{2,0,1:T(8,128)S(1)} %get-tuple-element.152, f32[128,16]{0,1:T(8,128)S(1)} %get-tuple-element.137, bf16[8192,256]{1,0:T(8,128)(2,1)} %get-tuple-element.168, s32[]{:T(128)S(6)} %select_n.46, ...), kind=kOutput, calls=%fused_computation.8.clone.1 | convolution fusion | flops 543686656 | bytes 10764296 | tf_op jit(solution)/shard_map/while/body/eval_jaxpr/thp,pd->thd/dot_general | solution.py:68
  152.6 2.2 bitcast_reduce_fusion.2
  156.2 2.9 %fusion.69 = f32[128,16,128]{2,0,1:T(8,128)S(1)} fusion(f32[1024,128,16]{1,0,2:T(8,128)S(1)} %get-tuple-element.135, f32[128,16]{0,1:T(8,128)S(1)} %max.4, f32[128,16,128]{2,0,1:T(8,128)S(1)} %get-tuple-element.152, f32[128,16]{0,1:T(8,128)S(1)} %get-tuple-element.137, bf16[8192,256]{1,0:T(8,128)(2,1)} %get-tuple-element.168, s32[]{:T(128)S(6)} %select_n.46, ...), kind=kOutput, calls=%fused_computation.8.clone.1 | convolution fusion | flops 543686656 | bytes 10764296 | tf_op jit(solution)/shard_map/while/body/eval_jaxpr/thp,pd->thd/dot_general | solution.py:68
  161.9 4.8 %fusion.51 = (f32[128]{0:T(128)S(1)}, f32[128,2048]{1,0:T(8,128)S(1)}) fusion(bf16[128,2048]{0,1:T(8,128)(2,1)S(1)} %bitcast.88, bf16[2048,2048]{1,0:T(8,128)(2,1)} %param.25, bf16[1,128,2048]{2,1,0:T(8,128)(2,1)S(1)} %copy-done.1), kind=kOutput, calls=%fused_computation.76 | convolution fusion | flops 1074528128 | bytes 10486272 | tf_op jit(solution)/shard_map/dot_general | solution.py:120
  168.2 45.8 %all-gather.7.cloned.1.call-done = bf16[1024,2048]{1,0:T(8,128)(2,1)} async-done(((bf16[128,2048]{1,0:T(8,128)(2,1)}), bf16[1024,2048]{1,0:T(8,128)(2,1)}) %all-gather.7.cloned.1.call-update) | async-done | bytes 4194320 | tf_op jit(solution)/shard_map/all_gather | solution.py:124
  214.0 15.1 %convolution_convert_fusion = bf16[1024,2048]{1,0:T(8,128)(2,1)} fusion(bf16[1024,2048]{1,0:T(8,128)(2,1)} %param.29, bf16[1024,2048]{1,0:T(8,128)(2,1)} %all-gather.7.cloned.1.call-done, bf16[2048,1024]{1,0:T(8,128)(2,1)} %param.28), kind=kOutput, calls=%fused_computation.25 | convolution fusion | flops 8601468928 | bytes 16777216 | tf_op jit(solution)/shard_map/dot_general | solution.py:131
  232.2 45.8 %reduce-scatter.2.cloned.1.call-done = bf16[128,2048]{1,0:T(8,128)(2,1)} async-done(((bf16[1024,2048]{1,0:T(8,128)(2,1)}), bf16[128,2048]{1,0:T(8,128)(2,1)}) %reduce-scatter.2.cloned.1.call-update) | async-done | bytes 524304 | tf_op jit(solution)/shard_map/reduce_scatter | solution.py:130
  278.0 2.0 fusion.39
  (79 shorter events, 20.9 us)
Async XLA Ops:
  6.5 50.4 %copy-start = (bf16[2048,256]{1,0:T(8,128)(2,1)S(1)}, bf16[2048,256]{1,0:T(8,128)(2,1)}, u32[]{:S(2)}) copy-start(bf16[2048,256]{1,0:T(8,128)(2,1)} %param.24) | copy-start | bytes 3145732
  6.5 40.7 %all-gather.5.cloned.1.call-start = ((), (), s32[]{:S(2)}) async-start(), calls=%async_computation.1 | async-start | bytes 2621440 | tf_op jit(solution)/shard_map/all_gather | solution.py:110
  7.3 89.2 %all-gather.9.cloned.1.call-start = ((), (), s32[]{:S(2)}) async-start(), calls=%async_computation.4 | async-start | bytes 4718592 | tf_op jit(solution)/shard_map/all_gather | solution.py:51
  49.1 164.9 %all-gather.7.cloned.1.call-start = ((), (), s32[]{:S(2)}) async-start(), calls=%async_computation.2 | async-start | bytes 4718592 | tf_op jit(solution)/shard_map/all_gather | solution.py:124
  51.7 5.2 %copy-start.1 = (bf16[1,128,2048]{2,1,0:T(8,128)(2,1)S(1)}, bf16[1,128,2048]{2,1,0:T(8,128)(2,1)}, u32[]{:S(2)}) copy-start(bf16[1,128,2048]{2,1,0:T(8,128)(2,1)} %param.16) | copy-start | bytes 1572868
  51.7 5.2 %copy-start.4 = (f32[2048]{0:T(1024)S(1)}, f32[2048]{0:T(1024)}, u32[]{:S(2)}) copy-start(f32[2048]{0:T(1024)} %param.22) | copy-start | bytes 24580
  51.8 5.2 %copy-start.5 = (f32[2048]{0:T(1024)S(1)}, f32[2048]{0:T(1024)}, u32[]{:S(2)}) copy-start(f32[2048]{0:T(1024)} %param.21) | copy-start | bytes 24580
  161.8 5.1 %copy-start.2 = (f32[2048]{0:T(1024)S(1)}, f32[2048]{0:T(1024)}, u32[]{:S(2)}) copy-start(f32[2048]{0:T(1024)} %param.27) | copy-start | bytes 24580
  161.9 5.1 %copy-start.3 = (f32[2048]{0:T(1024)S(1)}, f32[2048]{0:T(1024)}, u32[]{:S(2)}) copy-start(f32[2048]{0:T(1024)} %param.26) | copy-start | bytes 24580
  168.0 110.1 %reduce-scatter.2.cloned.1.call-start = ((), (), s32[]{:S(2)}) async-start(), calls=%async_computation.3 | async-start | bytes 4718592 | tf_op jit(solution)/shard_map/reduce_scatter | solution.py:130
  229.1 0.7 copy-start.6
  229.1 1.3 copy-start.7
Sparse Core Ops, SparseCore 0:
  9.2 38.0 all-gather.4
  49.3 47.1 all-gather.8
  168.1 45.8 all-gather.6
  229.3 48.7 reduce-scatter.1
where the time goes:
time: 288 us; the launch traced here: 287 us
  waiting for transfers between devices  167 us (58%)
  matrix products  67.1 us (23%)
  other arithmetic  22.2 us (8%)
  between operations  15.2 us (5%)
  local copies, waits for them, and re-layouts  8.7 us (3%)
  loops' own time  5.68 us (2%)
    reduce_scatter x1, waiting for transfers between devices, shards(): lax.psum_scatter(jnp.dot(hidden, contract_weight, preferred_element_type=...  45.8 us
    all_gather x1, waiting for transfers between devices, shards(): lax.all_gather(second, 'member', axis=0, tiled=True)  45.8 us
    all_gather x1, waiting for transfers between devices, folded_attention(): portion = lax.all_gather(selected, 'member', axis=0, tiled=True)  38.3 us
    all_gather x1, waiting for transfers between devices, shards(): every_block = lax.all_gather(prefix_cache, 'group', axis=0, tiled=True)  36.7 us
    dot_general x8, matrix products, advance(): jnp.einsum('thp,pd->thd', exponent.astype(jnp.bfloat16), key_block[:, hea...  23.5 us
    dot_general x8, matrix products, advance(): jnp.einsum('thd,pd->thp', queries, key_block[:, :head_size], preferred_el...  17.7 us
    dot_general x1, matrix products, shards(): jnp.dot(hidden, contract_weight, preferred_element_type=jnp.float32)  15.1 us
    reduce_sum x8, other arithmetic, advance(): denominator_next = denominator_now * rescale + jnp.sum(exponent, axis=-1)  11 us
  transfers between devices with their start and end apart: 4, of which 4 were waited for; matrix products, arithmetic and copies ran while one was open for 4% of the time, Pallas kernels for 0%

commit v1 on v0

--- a/solution.py
+++ b/solution.py
@@ -48,7 +48,26 @@
         preferred_element_type=jnp.float32,
     )
     running = (weighted, highest, denominator)
-    portion = lax.all_gather(selected, "member", axis=0, tiled=True)
+    prior = jax.lax.axis_size("member")
+    carry_out, small, earlier = (prior, jax.lax.axis_index("member"), selected.shape[0])
+    chunks = [(q, (q + 1) % carry_out) for q in range(carry_out)]
+    rack = [(q, (q - 1) % carry_out) for q in range(carry_out)]
+    portion = jnp.zeros(
+        (*selected.shape[:0], carry_out * earlier, *selected.shape[0 + 1 :]), selected.dtype
+    )
+    portion = lax.dynamic_update_slice_in_dim(portion, selected, small * earlier, axis=0)
+    inter = h_now = selected
+    r2 = carry_out // 2
+    for d in tuple(range(1, r2 + 1)):
+        inter = jax.lax.ppermute(inter, axis_name="member", perm=chunks)
+        portion = lax.dynamic_update_slice_in_dim(
+            portion, inter, (small - d) % carry_out * earlier, axis=0
+        )
+        if d < carry_out - r2:
+            h_now = jax.lax.ppermute(h_now, perm=rack, axis_name="member")
+            portion = lax.dynamic_update_slice_in_dim(
+                portion, h_now, (small + d) % carry_out * earlier, axis=0
+            )
     extent = portion.shape[0]
     stride = math.gcd(extent, 1024)
 

time: 288 us -> 295 us (1.024)
  waiting for transfers between devices: 167 us -> 152 us
  local copies, waits for them, and re-layouts: 8.7 us -> 19.6 us
  starting transfers between devices: 0.31 us -> 11.1 us
    all_gather x1 -> x0, waiting for transfers between devices: 38.3 us -> none  [folded_attention(): portion = lax.all_gather(selected, 'member', axis=0, tiled=True)]
    ppermute x0 -> x7, waiting for transfers between devices: none -> 26.9 us  [the longest x4 26.9 us: folded_attention(): inter = jax.lax.ppermute(inter, axis_name='member', perm=chunks)]
    dynamic_update_slice x0 -> x8, local copies, waits for them, and re-layouts: none -> 11.2 us  [the longest x4 5.43 us: folded_attention(): lax.dynamic_update_slice_in_dim(portion, inter, (small - d) % carry_out *...]
    ppermute x0 -> x7, starting transfers between devices: none -> 10.8 us  [the longest x3 10.7 us: folded_attention(): h_now = jax.lax.ppermute(h_now, perm=rack, axis_name='member')]
  transfers between devices with their start and end apart: 4 -> 10, of which waited for: 4 -> 7; matrix products, arithmetic and copies ran while one was open for 4% -> 8% of each run, Pallas kernels for 0% -> 0%
where the time goes in v1:
time: 295 us; the launch traced here: 294 us
  waiting for transfers between devices  152 us (52%)
  matrix products  68.1 us (23%)
  other arithmetic  22.2 us (8%)
  local copies, waits for them, and re-layouts  19.6 us (7%)
  between operations  15.4 us (5%)
  starting transfers between devices  11.1 us (4%)
  loops' own time  5.68 us (2%)
    reduce_scatter x1, waiting for transfers between devices, shards(): lax.psum_scatter(jnp.dot(hidden, contract_weight, preferred_element_type=...  45.8 us
    all_gather x1, waiting for transfers between devices, shards(): lax.all_gather(second, 'member', axis=0, tiled=True)  44.3 us
    all_gather x1, waiting for transfers between devices, shards(): every_block = lax.all_gather(prefix_cache, 'group', axis=0, tiled=True)  34.2 us
    ppermute x4, waiting for transfers between devices, folded_attention(): inter = jax.lax.ppermute(inter, axis_name='member', perm=chunks)  26.9 us
    dot_general x8, matrix products, advance(): jnp.einsum('thp,pd->thd', exponent.astype(jnp.bfloat16), key_block[:, hea...  23.5 us
    dot_general x8, matrix products, advance(): jnp.einsum('thd,pd->thp', queries, key_block[:, :head_size], preferred_el...  17.7 us
    dot_general x1, matrix products, shards(): jnp.dot(hidden, contract_weight, preferred_element_type=jnp.float32)  15.1 us
    reduce_sum x8, other arithmetic, advance(): denominator_next = denominator_now * rescale + jnp.sum(exponent, axis=-1)  11 us
  transfers between devices with their start and end apart: 10, of which 7 were waited for; matrix products, arithmetic and copies ran while one was open for 8% of the time, Pallas kernels for 0%

profile of v1, /device:TPU:0, one launch (start us, length us, event | category | flops | bytes accessed | tf_op | source)
XLA Modules:
  0.0 293.9 jit_solution(3526777746959075713)
XLA Ops:
  13.1 34.2 %all-gather.3.cloned.1.call-done = bf16[4,1024,256]{2,1,0:T(8,128)(2,1)} async-done(((bf16[1,1024,256]{2,1,0:T(8,128)(2,1)}), bf16[4,1024,256]{2,1,0:T(8,128)(2,1)}) %all-gather.3.cloned.1.call-update) | async-done | bytes 2097168 | tf_op jit(solution)/shard_map/all_gather | solution.py:129
  48.7 3.5 %collective-permute-start.1 = (bf16[1024,256]{1,0:T(8,128)(2,1)S(1)}, bf16[1024,256]{1,0:T(8,128)(2,1)}, u32[]{:S(2)}, u32[]{:S(2)}) collective-permute-start(bf16[1024,256]{1,0:T(8,128)(2,1)S(1)} %get-tuple-element.83), channel_id=1, source_target_pairs={{0,7},{1,0},{2,1},{3,2},{4,3},{5,4},{6,5},{7,6},{8,15},{9,8},{10,9... | collective-permute-start | bytes 1572872 | tf_op jit(solution)/shard_map/ppermute | solution.py:67
  52.3 4.7 %fusion.30 = bf16[16,16,8,128]{3,2,1,0:T(8,128)(2,1)S(1)} fusion(bf16[2048,2048]{1,0:T(8,128)(2,1)} %param.23, bf16[1,128,2048]{2,1,0:T(8,128)(2,1)S(1)} %copy-done.2, f32[2048]{0:T(1024)S(1)} %copy-done.7, f32[2048]{0:T(1024)S(1)} %copy-done.8, f32[128]{0:T(128)S(1)} %add_rsqrt_fusion.1, f32[128]{0:T(128)S(1)} %broadcast_multiply_fusion.1), kind=kOutput, calls=%fused_computation.39 | convolution fusion | flops 1075576832 | bytes 9454592 | tf_op jit(solution)/shard_map/dot_general | solution.py:133
  57.1 5.9 %collective-permute-done = bf16[1024,256]{1,0:T(8,128)(2,1)} collective-permute-done((bf16[1024,256]{1,0:T(8,128)(2,1)S(1)}, bf16[1024,256]{1,0:T(8,128)(2,1)}, u32[]{:S(2)}, u32[]{:S(2)}) %collective-permute-start) | collective-permute-done | bytes 524320 | tf_op jit(solution)/shard_map/ppermute | solution.py:62
  63.4 3.6 %collective-permute-start.3 = (bf16[1024,256]{1,0:T(8,128)(2,1)}, bf16[1024,256]{1,0:T(8,128)(2,1)}, u32[]{:S(2)}, u32[]{:S(2)}) collective-permute-start(bf16[1024,256]{1,0:T(8,128)(2,1)} %collective-permute-done.1), channel_id=1, source_target_pairs={{0,7},{1,0},{2,1},{3,2},{4,3},{5,4},{6,5},{7,6},{8,15},{9,8},{10,9... | collective-permute-start | bytes 1572872 | tf_op jit(solution)/shard_map/ppermute | solution.py:67
  68.9 10.3 %collective-permute-done.2 = bf16[1024,256]{1,0:T(8,128)(2,1)} collective-permute-done((bf16[1024,256]{1,0:T(8,128)(2,1)}, bf16[1024,256]{1,0:T(8,128)(2,1)}, u32[]{:S(2)}, u32[]{:S(2)}) %collective-permute-start.2) | collective-permute-done | bytes 524320 | tf_op jit(solution)/shard_map/ppermute | solution.py:62
  81.0 3.6 %collective-permute-start.5 = (bf16[1024,256]{1,0:T(8,128)(2,1)}, bf16[1024,256]{1,0:T(8,128)(2,1)S(1)}, u32[]{:S(2)}, u32[]{:S(2)}) collective-permute-start(bf16[1024,256]{1,0:T(8,128)(2,1)} %collective-permute-done.3), channel_id=1, source_target_pairs={{0,7},{1,0},{2,1},{3,2},{4,3},{5,4},{6,5},{7,6},{8,15},{9,8},{10,9... | collective-permute-start | bytes 1572872 | tf_op jit(solution)/shard_map/ppermute | solution.py:67
  86.4 7.6 %collective-permute-done.4 = bf16[1024,256]{1,0:T(8,128)(2,1)S(1)} collective-permute-done((bf16[1024,256]{1,0:T(8,128)(2,1)}, bf16[1024,256]{1,0:T(8,128)(2,1)S(1)}, u32[]{:S(2)}, u32[]{:S(2)}) %collective-permute-start.4) | collective-permute-done | bytes 524320 | tf_op jit(solution)/shard_map/ppermute | solution.py:62
  97.8 1.9 constant_dynamic-update-slice_fusion.3
  101.4 3.1 %collective-permute-done.6 = bf16[1024,256]{1,0:T(8,128)(2,1)S(1)} collective-permute-done((bf16[1024,256]{1,0:T(8,128)(2,1)S(1)}, bf16[1024,256]{1,0:T(8,128)(2,1)S(1)}, u32[]{:S(2)}, u32[]{:S(2)}) %collective-permute-start.6) | collective-permute-done | bytes 524320 | tf_op jit(solution)/shard_map/ppermute | solution.py:62
  105.3 62.7 %while.14 = (s32[]{:T(128)}, f32[128,16,128]{2,0,1:T(8,128)S(1)}, f32[128,16]{0,1:T(8,128)S(1)}, f32[128,16]{0,1:T(8,128)S(1)}, s32[8]{0:T(128)S(1)}, /*index=5*...) while((s32[]{:T(128)}, f32[128,16,128]{2,0,1:T(8,128)S(1)}, ...), condition=%wide.region_10.11_spmd, body=%wide.region_7.10_spmd.sunk | while | flops 1091047424 | bytes 28442832 | solution.py:95
  106.5 2.2 bitcast_reduce_fusion.2
  110.1 2.9 %fusion.69 = f32[128,16,128]{2,0,1:T(8,128)S(1)} fusion(f32[1024,128,16]{1,0,2:T(8,128)S(1)} %get-tuple-element.137, f32[128,16]{0,1:T(8,128)S(1)} %max.4, f32[128,16,128]{2,0,1:T(8,128)S(1)} %get-tuple-element.154, f32[128,16]{0,1:T(8,128)S(1)} %get-tuple-element.139, bf16[8192,256]{1,0:T(8,128)(2,1)} %get-tuple-element.170, s32[]{:T(128)S(6)} %select_n.116, ...), kind=kOutput, calls=%fused_computation.8.clone.1 | convolution fusion | flops 543686656 | bytes 10764296 | tf_op jit(solution)/shard_map/while/body/eval_jaxpr/thp,pd->thd/dot_general | solution.py:87
  114.4 2.2 bitcast_reduce_fusion.2
  118.0 2.9 %fusion.69 = f32[128,16,128]{2,0,1:T(8,128)S(1)} fusion(f32[1024,128,16]{1,0,2:T(8,128)S(1)} %get-tuple-element.137, f32[128,16]{0,1:T(8,128)S(1)} %max.4, f32[128,16,128]{2,0,1:T(8,128)S(1)} %get-tuple-element.154, f32[128,16]{0,1:T(8,128)S(1)} %get-tuple-element.139, bf16[8192,256]{1,0:T(8,128)(2,1)} %get-tuple-element.170, s32[]{:T(128)S(6)} %select_n.116, ...), kind=kOutput, calls=%fused_computation.8.clone.1 | convolution fusion | flops 543686656 | bytes 10764296 | tf_op jit(solution)/shard_map/while/body/eval_jaxpr/thp,pd->thd/dot_general | solution.py:87
  122.2 2.2 bitcast_reduce_fusion.2
  125.8 2.9 %fusion.69 = f32[128,16,128]{2,0,1:T(8,128)S(1)} fusion(f32[1024,128,16]{1,0,2:T(8,128)S(1)} %get-tuple-element.137, f32[128,16]{0,1:T(8,128)S(1)} %max.4, f32[128,16,128]{2,0,1:T(8,128)S(1)} %get-tuple-element.154, f32[128,16]{0,1:T(8,128)S(1)} %get-tuple-element.139, bf16[8192,256]{1,0:T(8,128)(2,1)} %get-tuple-element.170, s32[]{:T(128)S(6)} %select_n.116, ...), kind=kOutput, calls=%fused_computation.8.clone.1 | convolution fusion | flops 543686656 | bytes 10764296 | tf_op jit(solution)/shard_map/while/body/eval_jaxpr/thp,pd->thd/dot_general | solution.py:87
  130.0 2.2 bitcast_reduce_fusion.2
  133.7 2.9 %fusion.69 = f32[128,16,128]{2,0,1:T(8,128)S(1)} fusion(f32[1024,128,16]{1,0,2:T(8,128)S(1)} %get-tuple-element.137, f32[128,16]{0,1:T(8,128)S(1)} %max.4, f32[128,16,128]{2,0,1:T(8,128)S(1)} %get-tuple-element.154, f32[128,16]{0,1:T(8,128)S(1)} %get-tuple-element.139, bf16[8192,256]{1,0:T(8,128)(2,1)} %get-tuple-element.170, s32[]{:T(128)S(6)} %select_n.116, ...), kind=kOutput, calls=%fused_computation.8.clone.1 | convolution fusion | flops 543686656 | bytes 10764296 | tf_op jit(solution)/shard_map/while/body/eval_jaxpr/thp,pd->thd/dot_general | solution.py:87
  137.9 2.2 bitcast_reduce_fusion.2
  141.5 2.9 %fusion.69 = f32[128,16,128]{2,0,1:T(8,128)S(1)} fusion(f32[1024,128,16]{1,0,2:T(8,128)S(1)} %get-tuple-element.137, f32[128,16]{0,1:T(8,128)S(1)} %max.4, f32[128,16,128]{2,0,1:T(8,128)S(1)} %get-tuple-element.154, f32[128,16]{0,1:T(8,128)S(1)} %get-tuple-element.139, bf16[8192,256]{1,0:T(8,128)(2,1)} %get-tuple-element.170, s32[]{:T(128)S(6)} %select_n.116, ...), kind=kOutput, calls=%fused_computation.8.clone.1 | convolution fusion | flops 543686656 | bytes 10764296 | tf_op jit(solution)/shard_map/while/body/eval_jaxpr/thp,pd->thd/dot_general | solution.py:87
  145.7 2.2 bitcast_reduce_fusion.2
  149.3 2.9 %fusion.69 = f32[128,16,128]{2,0,1:T(8,128)S(1)} fusion(f32[1024,128,16]{1,0,2:T(8,128)S(1)} %get-tuple-element.137, f32[128,16]{0,1:T(8,128)S(1)} %max.4, f32[128,16,128]{2,0,1:T(8,128)S(1)} %get-tuple-element.154, f32[128,16]{0,1:T(8,128)S(1)} %get-tuple-element.139, bf16[8192,256]{1,0:T(8,128)(2,1)} %get-tuple-element.170, s32[]{:T(128)S(6)} %select_n.116, ...), kind=kOutput, calls=%fused_computation.8.clone.1 | convolution fusion | flops 543686656 | bytes 10764296 | tf_op jit(solution)/shard_map/while/body/eval_jaxpr/thp,pd->thd/dot_general | solution.py:87
  153.6 2.2 bitcast_reduce_fusion.2
  157.2 2.9 %fusion.69 = f32[128,16,128]{2,0,1:T(8,128)S(1)} fusion(f32[1024,128,16]{1,0,2:T(8,128)S(1)} %get-tuple-element.137, f32[128,16]{0,1:T(8,128)S(1)} %max.4, f32[128,16,128]{2,0,1:T(8,128)S(1)} %get-tuple-element.154, f32[128,16]{0,1:T(8,128)S(1)} %get-tuple-element.139, bf16[8192,256]{1,0:T(8,128)(2,1)} %get-tuple-element.170, s32[]{:T(128)S(6)} %select_n.116, ...), kind=kOutput, calls=%fused_computation.8.clone.1 | convolution fusion | flops 543686656 | bytes 10764296 | tf_op jit(solution)/shard_map/while/body/eval_jaxpr/thp,pd->thd/dot_general | solution.py:87
  161.4 2.2 bitcast_reduce_fusion.2
  165.0 2.9 %fusion.69 = f32[128,16,128]{2,0,1:T(8,128)S(1)} fusion(f32[1024,128,16]{1,0,2:T(8,128)S(1)} %get-tuple-element.137, f32[128,16]{0,1:T(8,128)S(1)} %max.4, f32[128,16,128]{2,0,1:T(8,128)S(1)} %get-tuple-element.154, f32[128,16]{0,1:T(8,128)S(1)} %get-tuple-element.139, bf16[8192,256]{1,0:T(8,128)(2,1)} %get-tuple-element.170, s32[]{:T(128)S(6)} %select_n.116, ...), kind=kOutput, calls=%fused_computation.8.clone.1 | convolution fusion | flops 543686656 | bytes 10764296 | tf_op jit(solution)/shard_map/while/body/eval_jaxpr/thp,pd->thd/dot_general | solution.py:87
  170.7 4.8 %fusion.51 = (f32[128]{0:T(128)S(1)}, f32[128,2048]{1,0:T(8,128)S(1)}) fusion(bf16[128,2048]{0,1:T(8,128)(2,1)S(1)} %bitcast.90, bf16[2048,2048]{1,0:T(8,128)(2,1)} %param.25, bf16[1,128,2048]{2,1,0:T(8,128)(2,1)S(1)} %copy-done.2), kind=kOutput, calls=%fused_computation.84 | convolution fusion | flops 1074528128 | bytes 10486272 | tf_op jit(solution)/shard_map/dot_general | solution.py:139
  177.1 44.3 %all-gather.5.cloned.1.call-done = bf16[1024,2048]{1,0:T(8,128)(2,1)} async-done(((bf16[128,2048]{1,0:T(8,128)(2,1)}), bf16[1024,2048]{1,0:T(8,128)(2,1)}) %all-gather.5.cloned.1.call-update) | async-done | bytes 4194320 | tf_op jit(solution)/shard_map/all_gather | solution.py:143
  221.4 15.1 %convolution_convert_fusion = bf16[1024,2048]{1,0:T(8,128)(2,1)} fusion(bf16[1024,2048]{1,0:T(8,128)(2,1)} %param.29, bf16[1024,2048]{1,0:T(8,128)(2,1)} %all-gather.5.cloned.1.call-done, bf16[2048,1024]{1,0:T(8,128)(2,1)} %param.28), kind=kOutput, calls=%fused_computation.25 | convolution fusion | flops 8601468928 | bytes 16777216 | tf_op jit(solution)/shard_map/dot_general | solution.py:150
  239.6 45.8 %reduce-scatter.2.cloned.1.call-done = bf16[128,2048]{1,0:T(8,128)(2,1)} async-done(((bf16[1024,2048]{1,0:T(8,128)(2,1)}), bf16[128,2048]{1,0:T(8,128)(2,1)}) %reduce-scatter.2.cloned.1.call-update) | async-done | bytes 524304 | tf_op jit(solution)/shard_map/reduce_scatter | solution.py:149
  285.4 2.0 fusion.39
  (104 shorter events, 41.2 us)
Async XLA Ops:
  6.5 56.4 %copy-start = (bf16[2048,256]{1,0:T(8,128)(2,1)S(1)}, bf16[2048,256]{1,0:T(8,128)(2,1)}, u32[]{:S(2)}) copy-start(bf16[2048,256]{1,0:T(8,128)(2,1)} %param.24) | copy-start | bytes 3145732
  6.5 45.7 %copy-start.2 = (bf16[1,128,2048]{2,1,0:T(8,128)(2,1)S(1)}, bf16[1,128,2048]{2,1,0:T(8,128)(2,1)}, u32[]{:S(2)}) copy-start(bf16[1,128,2048]{2,1,0:T(8,128)(2,1)} %param.16) | copy-start | bytes 1572868
  6.5 45.7 %copy-start.7 = (f32[2048]{0:T(1024)S(1)}, f32[2048]{0:T(1024)}, u32[]{:S(2)}) copy-start(f32[2048]{0:T(1024)} %param.22) | copy-start | bytes 24580
  6.5 45.7 %copy-start.8 = (f32[2048]{0:T(1024)S(1)}, f32[2048]{0:T(1024)}, u32[]{:S(2)}) copy-start(f32[2048]{0:T(1024)} %param.21) | copy-start | bytes 24580
  6.5 40.7 %all-gather.3.cloned.1.call-start = ((), (), s32[]{:S(2)}) async-start(), calls=%async_computation.1 | async-start | bytes 2621440 | tf_op jit(solution)/shard_map/all_gather | solution.py:129
  7.3 214.1 %all-gather.5.cloned.1.call-start = ((), (), s32[]{:S(2)}) async-start(), calls=%async_computation.2 | async-start | bytes 4718592 | tf_op jit(solution)/shard_map/all_gather | solution.py:143
  48.7 8.3 %copy-start.1 = (bf16[8192,256]{1,0:T(8,128)(2,1)}, bf16[8192,256]{1,0:T(8,128)(2,1)S(1)}, u32[]{:S(2)}) copy-start(bf16[8192,256]{1,0:T(8,128)(2,1)S(1)} %get-tuple-element.82) | copy-start | bytes 12582916
  48.7 14.3 %collective-permute-start = (bf16[1024,256]{1,0:T(8,128)(2,1)S(1)}, bf16[1024,256]{1,0:T(8,128)(2,1)}, u32[]{:S(2)}, u32[]{:S(2)}) collective-permute-start(bf16[1024,256]{1,0:T(8,128)(2,1)S(1)} %get-tuple-element.83), channel_id=1, source_target_pairs={{0,1},{1,2},{2,3},{3,4},{4,5},{5,6},{6,7},{7,0},{8,9},{9,10},{10,1... | collective-permute-start | bytes 1572872 | tf_op jit(solution)/shard_map/ppermute | solution.py:62
  48.7 14.6 %collective-permute-start.1 = (bf16[1024,256]{1,0:T(8,128)(2,1)S(1)}, bf16[1024,256]{1,0:T(8,128)(2,1)}, u32[]{:S(2)}, u32[]{:S(2)}) collective-permute-start(bf16[1024,256]{1,0:T(8,128)(2,1)S(1)} %get-tuple-element.83), channel_id=1, source_target_pairs={{0,7},{1,0},{2,1},{3,2},{4,3},{5,4},{6,5},{7,6},{8,15},{9,8},{10,9... | collective-permute-start | bytes 1572872 | tf_op jit(solution)/shard_map/ppermute | solution.py:67
  57.0 10.4 %copy-start.4 = (bf16[16,16,8,128]{3,2,1,0:T(8,128)(2,1)}, bf16[16,16,8,128]{3,2,1,0:T(8,128)(2,1)S(1)}, u32[]{:S(2)}) copy-start(bf16[16,16,8,128]{3,2,1,0:T(8,128)(2,1)S(1)} %fusion.30) | copy-start | bytes 1572868
  63.0 16.2 %collective-permute-start.2 = (bf16[1024,256]{1,0:T(8,128)(2,1)}, bf16[1024,256]{1,0:T(8,128)(2,1)}, u32[]{:S(2)}, u32[]{:S(2)}) collective-permute-start(bf16[1024,256]{1,0:T(8,128)(2,1)} %collective-permute-done), channel_id=1, source_target_pairs={{0,1},{1,2},{2,3},{3,4},{4,5},{5,6},{6,7},{7,0},{8,9},{9,10},{10,1... | collective-permute-start | bytes 1572872 | tf_op jit(solution)/shard_map/ppermute | solution.py:62
  63.4 17.6 %collective-permute-start.3 = (bf16[1024,256]{1,0:T(8,128)(2,1)}, bf16[1024,256]{1,0:T(8,128)(2,1)}, u32[]{:S(2)}, u32[]{:S(2)}) collective-permute-start(bf16[1024,256]{1,0:T(8,128)(2,1)} %collective-permute-done.1), channel_id=1, source_target_pairs={{0,7},{1,0},{2,1},{3,2},{4,3},{5,4},{6,5},{7,6},{8,15},{9,8},{10,9... | collective-permute-start | bytes 1572872 | tf_op jit(solution)/shard_map/ppermute | solution.py:67
  67.3 11.9 %copy-start.3 = (f32[128,16,128]{0,2,1:T(8,128)}, f32[128,16,128]{0,2,1:T(8,128)S(1)}, u32[]{:S(2)}) copy-start(f32[128,16,128]{0,2,1:T(8,128)S(1)} %get-tuple-element.87) | copy-start | bytes 3145732
  79.2 14.8 %collective-permute-start.4 = (bf16[1024,256]{1,0:T(8,128)(2,1)}, bf16[1024,256]{1,0:T(8,128)(2,1)S(1)}, u32[]{:S(2)}, u32[]{:S(2)}) collective-permute-start(bf16[1024,256]{1,0:T(8,128)(2,1)} %collective-permute-done.2), channel_id=1, source_target_pairs={{0,1},{1,2},{2,3},{3,4},{4,5},{5,6},{6,7},{7,0},{8,9},{9,10},{10,1... | collective-permute-start | bytes 1572872 | tf_op jit(solution)/shard_map/ppermute | solution.py:62
  81.0 19.6 %collective-permute-start.5 = (bf16[1024,256]{1,0:T(8,128)(2,1)}, bf16[1024,256]{1,0:T(8,128)(2,1)S(1)}, u32[]{:S(2)}, u32[]{:S(2)}) collective-permute-start(bf16[1024,256]{1,0:T(8,128)(2,1)} %collective-permute-done.3), channel_id=1, source_target_pairs={{0,7},{1,0},{2,1},{3,2},{4,3},{5,4},{6,5},{7,6},{8,15},{9,8},{10,9... | collective-permute-start | bytes 1572872 | tf_op jit(solution)/shard_map/ppermute | solution.py:67
  94.0 10.4 %collective-permute-start.6 = (bf16[1024,256]{1,0:T(8,128)(2,1)S(1)}, bf16[1024,256]{1,0:T(8,128)(2,1)S(1)}, u32[]{:S(2)}, u32[]{:S(2)}) collective-permute-start(bf16[1024,256]{1,0:T(8,128)(2,1)S(1)} %collective-permute-done.4), channel_id=1, source_target_pairs={{0,1},{1,2},{2,3},{3,4},{4,5},{5,6},{6,7},{7,0},{8,9},{9,10},{10,1... | collective-permute-start | bytes 1572872 | tf_op jit(solution)/shard_map/ppermute | solution.py:62
  170.7 5.1 %copy-start.5 = (f32[2048]{0:T(1024)S(1)}, f32[2048]{0:T(1024)}, u32[]{:S(2)}) copy-start(f32[2048]{0:T(1024)} %param.27) | copy-start | bytes 24580
  170.7 5.1 %copy-start.6 = (f32[2048]{0:T(1024)S(1)}, f32[2048]{0:T(1024)}, u32[]{:S(2)}) copy-start(f32[2048]{0:T(1024)} %param.26) | copy-start | bytes 24580
  176.8 108.6 %reduce-scatter.2.cloned.1.call-start = ((), (), s32[]{:S(2)}) async-start(), calls=%async_computation.3 | async-start | bytes 4718592 | tf_op jit(solution)/shard_map/reduce_scatter | solution.py:149
  236.5 0.7 copy-start.9
  236.5 1.3 copy-start.10
Sparse Core Ops, SparseCore 0:
  9.2 38.0 all-gather.2
  176.9 44.4 all-gather.4
  236.7 48.7 reduce-scatter.1
